TPU v7x, 512 devices: a whole 4x8x8 slice. The times are simulated.
512 devices in a mesh: dp: 32 (over y_lo, z), fsdp: 16 (over x, y_hi, core).
Axes of the slice: x: 4, y: 8 (y_hi: 2, y_lo: 4; y = y_hi * 4 + y_lo), z: 8, core: 2. Of those that a mesh axis runs over, the one named last changes fastest.
Arguments:
- tokens: bfloat16 [65536, 2048], P(('dp', 'fsdp')), may hold values from -6 to 6
- upstream: bfloat16 [65536, 512], P(('dp', 'fsdp')), may hold values from -6 to 6
- value_weight: bfloat16 [2048, 512], P('fsdp'), may hold values from -0.125 to 0.125
- forget_label: int32 [32], P('dp'), may hold values 0 or 1
- copy_index: int32 [32], P('dp'), may hold values from 0 to 1, as said below
- adv_rate: float32 [2], replicated, may hold values from 0.5 to 2
Outputs:
- meta_grad: float32 [2048, 512], P('fsdp')
Inputs may be any that keep to these rules, and one draw needn't show every extreme that they name: `copy_index`: each of the 2 copies is named by exactly 16 sequences.
All inputs are finite; a program needn't handle non-finite values. No bound on the sum of `forget_label` on one device may be relied on, other than what follows from the above.
Results may differ from a plain program's by a relative error of at most 0.0056.
Values may be sent and summed in bfloat16 or wider, within the bound.
A program may use at most 64 MiB of HBM per device.

v0:
```python
import jax
import jax.numpy as jnp
from jax import lax
from jax.sharding import PartitionSpec as P


def first_slope(value):
    sig = jax.nn.sigmoid(value)
    return sig * (1.0 + value * (1.0 - sig))


def second_slope(value):
    sig = jax.nn.sigmoid(value)
    return sig * (1.0 - sig) * (2.0 + value * (1.0 - 2.0 * sig))


def local(tokens, upstream, value_weight, forget_label, copy_index, adv_rate):
    groups = lax.axis_size("fsdp")
    seq_count = lax.axis_size("dp")
    seq_length = tokens.shape[0] * groups
    forget = forget_label[0].astype(jnp.float32)
    onehot = (jnp.arange(adv_rate.shape[0], dtype=jnp.int32) == copy_index[0]).astype(jnp.float32)
    own_rate = jnp.sum(onehot * adv_rate)
    upward = upstream.astype(jnp.float32)

    def project(piece):
        return jnp.dot(tokens, piece, preferred_element_type=jnp.float32)

    primal = project(lax.all_gather(value_weight, "fsdp", axis=0, tiled=True))
    columns = lax.all_to_all(tokens, "fsdp", split_axis=1, concat_axis=0, tiled=True)

    def contract(piece):
        return lax.dot_general(
            columns, piece, (((0,), (0,)), ((), ())), preferred_element_type=jnp.float32
        )

    delta_adv = (forget * upward * first_slope(primal) / seq_length).astype(jnp.bfloat16)
    grad_local = lax.psum_scatter(
        lax.dot_general(
            tokens, delta_adv, (((0,), (0,)), ((), ())), preferred_element_type=jnp.float32
        ),
        "fsdp",
        scatter_dimension=0,
        tiled=True,
    )
    stacked = lax.psum(onehot[:, None, None] * grad_local[None], "dp")
    grad_own = jnp.sum(onehot[:, None, None] * stacked, axis=0)
    attacked = (value_weight.astype(jnp.float32) - own_rate * grad_own).astype(jnp.bfloat16)
    altered = project(lax.all_gather(attacked, "fsdp", axis=0, tiled=True))
    delta_out = ((1.0 - 2.0 * forget) * upward * first_slope(altered) / seq_length).astype(
        jnp.bfloat16
    )
    outer_local = contract(lax.all_gather(delta_out, "fsdp", axis=0, tiled=True))
    outer_all = lax.psum(onehot[:, None, None] * outer_local[None], "dp")
    tangent = jnp.sum(onehot[:, None, None] * outer_all, axis=0).astype(jnp.bfloat16)
    forward_tangent = project(lax.all_gather(tangent, "fsdp", axis=0, tiled=True))
    delta_curv = (forget * upward * second_slope(primal) * forward_tangent / seq_length).astype(
        jnp.bfloat16
    )
    curv_local = contract(lax.all_gather(delta_curv, "fsdp", axis=0, tiled=True))
    curv_sum = lax.psum(own_rate * curv_local, "dp")
    scale = (float(seq_length) / float(seq_count)) ** 0.5
    return scale * (jnp.sum(outer_all, axis=0) - curv_sum)


def solution(mesh):
    in_specs = (
        P(("dp", "fsdp"), None),
        P(("dp", "fsdp"), None),
        P("fsdp", None),
        P("dp"),
        P("dp"),
        P(),
    )
    out_specs = P("fsdp", None)
    return jax.shard_map(local, mesh=mesh, in_specs=in_specs, out_specs=out_specs, check_vma=False)
```

profile of v0, /device:TPU:2, one launch (start us, length us, event | category | flops | bytes accessed | tf_op | source)
XLA Modules:
  0.0 1404.9 jit_solution(12837787341775304741)
XLA Ops:
  8.0 71.3 %all-gather.6.cloned.1.call-done = bf16[2048,512]{1,0:T(8,128)(2,1)} async-done(((bf16[128,512]{1,0:T(8,128)(2,1)}), bf16[2048,512]{1,0:T(8,128)(2,1)}) %all-gather.6.cloned.1.call-update) | async-done | bytes 2097168 | tf_op jit(solution)/shard_map/all_gather | solution.py:29
  79.3 2.2 fusion.21
  81.5 2.7 convolution_bitcast_fusion
  85.0 108.9 %reduce-scatter.2.cloned.1.call-done = f32[128,512]{0,1:T(8,128)} async-done(((f32[2048,512]{0,1:T(8,128)}), f32[128,512]{0,1:T(8,128)}) %reduce-scatter.2.cloned.1.call-update) | async-done | bytes 262160 | tf_op jit(solution)/shard_map/reduce_scatter | solution.py:38
  193.9 1.1 copy.20
  195.0 0.9 broadcast_multiply_fusion.1
  196.7 309.2 %all-reduce.4.cloned.1.call-done = f32[2,128,512]{2,1,0:T(8,128)} async-done(((f32[2,128,512]{2,1,0:T(8,128)}), f32[2,128,512]{2,1,0:T(8,128)}) %all-reduce.4.cloned.1.call-update) | async-done | bytes 524304 | tf_op jit(solution)/shard_map/psum | solution.py:46
  505.9 1.2 multiply_reduce_fusion.1
  507.1 1.3 subtract_convert_fusion
  508.5 59.6 %all-gather.8.cloned.1.call-done = bf16[2048,512]{1,0:T(8,128)(2,1)} async-done(((bf16[128,512]{1,0:T(8,128)(2,1)}), bf16[2048,512]{1,0:T(8,128)(2,1)}) %all-gather.8.cloned.1.call-update) | async-done | bytes 2097168 | tf_op jit(solution)/shard_map/all_gather | solution.py:49
  568.0 2.8 fusion.10
  571.1 21.9 %all_to_all.19 = bf16[128,16,128]{0,2,1:T(8,128)(2,1)S(1)} all-to-all(bf16[128,16,128]{0,2,1:T(8,128)(2,1)S(1)} %bitcast.39), channel_id=1, replica_groups=mesh['dp'=32,'fsdp'=16] {'fsdp'}, dimensions={1} | all-to-all | bytes 1048576 | tf_op jit(solution)/shard_map/all_to_all | solution.py:30
  593.3 46.8 %all-gather.10.cloned.1.call-done = bf16[2048,512]{1,0:T(8,128)(2,1)} async-done(((bf16[128,512]{1,0:T(8,128)(2,1)}), bf16[2048,512]{1,0:T(8,128)(2,1)}) %all-gather.10.cloned.1.call-update) | async-done | bytes 2097168 | tf_op jit(solution)/shard_map/all_gather | solution.py:53
  640.1 2.3 convolution_bitcast_fusion.3
  642.6 0.9 broadcast_multiply_fusion
  643.6 310.1 %all-reduce.6.cloned.1.call-done = f32[2,128,512]{2,1,0:T(8,128)} async-done(((f32[2,128,512]{2,1,0:T(8,128)}), f32[2,128,512]{2,1,0:T(8,128)}) %all-reduce.6.cloned.1.call-update) | async-done | bytes 524304 | tf_op jit(solution)/shard_map/psum | solution.py:54
  953.7 1.9 multiply_reduce_fusion
  955.6 60.4 %all-gather.12.cloned.1.call-done = bf16[2048,512]{1,0:T(8,128)(2,1)} async-done(((bf16[128,512]{1,0:T(8,128)(2,1)}), bf16[2048,512]{1,0:T(8,128)(2,1)}) %all-gather.12.cloned.1.call-update) | async-done | bytes 2097168 | tf_op jit(solution)/shard_map/all_gather | solution.py:56
  1016.0 2.7 fusion.3
  1018.8 64.4 %all-gather.14.cloned.1.call-done = bf16[2048,512]{1,0:T(8,128)(2,1)} async-done(((bf16[128,512]{1,0:T(8,128)(2,1)}), bf16[2048,512]{1,0:T(8,128)(2,1)}) %all-gather.14.cloned.1.call-update) | async-done | bytes 2097168 | tf_op jit(solution)/shard_map/all_gather | solution.py:60
  1083.2 3.7 fusion.2
  1087.0 309.6 %all-reduce.8.cloned.1.call-done = f32[128,512]{0,1:T(8,128)} async-done(((f32[128,512]{0,1:T(8,128)}), f32[128,512]{0,1:T(8,128)}) %all-reduce.8.cloned.1.call-update) | async-done | bytes 262160 | tf_op jit(solution)/shard_map/psum | solution.py:61
  1396.5 1.0 subtract_multiply_fusion.2
  1397.5 0.8 copy.27
  (32 shorter events, 2.7 us)
Async XLA Ops:
  6.5 75.0 %copy-start = (bf16[128,2048]{1,0:T(8,128)(2,1)S(1)}, bf16[128,2048]{1,0:T(8,128)(2,1)}, u32[]{:S(2)}) copy-start(bf16[128,2048]{1,0:T(8,128)(2,1)} %param.6) | copy-start | bytes 1572868
  6.5 75.0 %copy-start.2 = (bf16[128,512]{1,0:T(8,128)(2,1)S(1)}, bf16[128,512]{1,0:T(8,128)(2,1)}, u32[]{:S(2)}) copy-start(bf16[128,512]{1,0:T(8,128)(2,1)} %param.7) | copy-start | bytes 393220
  6.5 72.8 %all-gather.6.cloned.1.call-start = ((), (), s32[]{:S(2)}) async-start(), calls=%async_computation.2 | async-start | bytes 2228224 | tf_op jit(solution)/shard_map/all_gather | solution.py:29
  7.3 186.6 %reduce-scatter.2.cloned.1.call-start = ((), (), s32[]{:S(2)}) async-start(), calls=%async_computation.3 | async-start | bytes 4456448 | tf_op jit(solution)/shard_map/reduce_scatter | solution.py:38
  84.2 111.8 %copy-start.3 = (f32[2]{0:T(128)S(1)}, f32[2]{0:T(128)}, u32[]{:S(2)}) copy-start(f32[2]{0:T(128)} %param.11) | copy-start | bytes 28
  84.3 422.8 %copy-start.1 = (bf16[128,512]{1,0:T(8,128)(2,1)S(1)}, bf16[128,512]{1,0:T(8,128)(2,1)}, u32[]{:S(2)}) copy-start(bf16[128,512]{1,0:T(8,128)(2,1)} %param.8) | copy-start | bytes 393220
  84.3 421.6 %all-reduce.4.cloned.1.call-start = ((), (), s32[]{:S(2)}) async-start(), calls=%async_computation.4 | async-start | bytes 1048576 | tf_op jit(solution)/shard_map/psum | solution.py:46
  195.9 372.1 %all-gather.8.cloned.1.call-start = ((), (), s32[]{:S(2)}) async-start(), calls=%async_computation.5 | async-start | bytes 2228224 | tf_op jit(solution)/shard_map/all_gather | solution.py:49
  508.4 131.7 %all-gather.10.cloned.1.call-start = ((), (), s32[]{:S(2)}) async-start(), calls=%async_computation.6 | async-start | bytes 2228224 | tf_op jit(solution)/shard_map/all_gather | solution.py:53
  570.8 382.9 %all-reduce.6.cloned.1.call-start = ((), (), s32[]{:S(2)}) async-start(), calls=%async_computation.7 | async-start | bytes 1048576 | tf_op jit(solution)/shard_map/psum | solution.py:54
  643.6 372.5 %all-gather.12.cloned.1.call-start = ((), (), s32[]{:S(2)}) async-start(), calls=%async_computation.8 | async-start | bytes 2228224 | tf_op jit(solution)/shard_map/all_gather | solution.py:56
  955.6 127.6 %all-gather.14.cloned.1.call-start = ((), (), s32[]{:S(2)}) async-start(), calls=%async_computation.9 | async-start | bytes 2228224 | tf_op jit(solution)/shard_map/all_gather | solution.py:60
  1018.8 377.8 %all-reduce.8.cloned.1.call-start = ((), (), s32[]{:S(2)}) async-start(), calls=%async_computation.10 | async-start | bytes 524288 | tf_op jit(solution)/shard_map/psum | solution.py:61
Sparse Core Ops, SparseCore 0:
  10.6 68.6 all-gather.5
  84.4 109.4 reduce-scatter.1
  196.8 309.0 all-reduce.3
  509.0 58.9 all-gather.7
  571.1 68.9 all-gather.9
  643.7 309.9 all-reduce.5
  957.0 58.9 all-gather.11
  1019.3 63.8 all-gather.13
  1087.0 309.5 all-reduce.7
where the time goes:
time: 1410 us; the launch traced here: 1400 us
  waiting for transfers between devices  1340 us (95%)
  blocking collectives  21.9 us (2%)
  matrix products  16.4 us (1%)
  between operations  14.6 us (1%)
    psum x1, waiting for transfers between devices, local(): outer_all = lax.psum(onehot[:, None, None] * outer_local[None], 'dp')  310 us
    psum x1, waiting for transfers between devices, local(): curv_sum = lax.psum(own_rate * curv_local, 'dp')  310 us
    psum x1, waiting for transfers between devices, local(): stacked = lax.psum(onehot[:, None, None] * grad_local[None], 'dp')  309 us
    reduce_scatter x1, waiting for transfers between devices, local(): lax.psum_scatter(lax.dot_general(tokens, delta_adv, (((0,), (0,)), ((), (...  109 us
    all_gather x1, waiting for transfers between devices, local(): primal = project(lax.all_gather(value_weight, 'fsdp', axis=0, tiled=True))  71.3 us
    all_gather x1, waiting for transfers between devices, local(): lax.all_gather(delta_curv, 'fsdp', axis=0, tiled=True)  64.4 us
    all_gather x1, waiting for transfers between devices, local(): lax.all_gather(tangent, 'fsdp', axis=0, tiled=True)  60.4 us
    all_gather x1, waiting for transfers between devices, local(): altered = project(lax.all_gather(attacked, 'fsdp', axis=0, tiled=True))  59.6 us
  transfers between devices with their start and end apart: 9, of which 9 were waited for; matrix products, arithmetic and copies ran while one was open for 0% of the time, Pallas kernels for 0%

commit v1 on v0

--- a/solution.py
+++ b/solution.py
@@ -58,7 +58,7 @@
         jnp.bfloat16
     )
     curv_local = contract(lax.all_gather(delta_curv, "fsdp", axis=0, tiled=True))
-    curv_sum = lax.psum(own_rate * curv_local, "dp")
+    curv_sum = jnp.sum(lax.all_gather(own_rate * curv_local, "dp"), axis=0)
     scale = (float(seq_length) / float(seq_count)) ** 0.5
     return scale * (jnp.sum(outer_all, axis=0) - curv_sum)
 

time: 1410 us -> 1270 us (0.901)
  the two profiles are of different devices: /device:TPU:2 before, /device:TPU:14 now
where the time goes in v1:
time: 1270 us
  waiting for transfers between devices  1200 us (94%)
  blocking collectives  23.3 us (2%)
  matrix products  16.4 us (1%)
  between operations  14.6 us (1%)
    psum x1, waiting for transfers between devices, local(): outer_all = lax.psum(onehot[:, None, None] * outer_local[None], 'dp')  299 us
    psum x1, waiting for transfers between devices, local(): stacked = lax.psum(onehot[:, None, None] * grad_local[None], 'dp')  299 us
    all_gather x1, waiting for transfers between devices, local(): curv_sum = jnp.sum(lax.all_gather(own_rate * curv_local, 'dp'), axis=0)  170 us
    reduce_scatter x1, waiting for transfers between devices, local(): lax.psum_scatter(lax.dot_general(tokens, delta_adv, (((0,), (0,)), ((), (...  108 us
    all_gather x1, waiting for transfers between devices, local(): primal = project(lax.all_gather(value_weight, 'fsdp', axis=0, tiled=True))  73.9 us
    all_gather x1, waiting for transfers between devices, local(): lax.all_gather(tangent, 'fsdp', axis=0, tiled=True)  71.8 us
    all_gather x1, waiting for transfers between devices, local(): altered = project(lax.all_gather(attacked, 'fsdp', axis=0, tiled=True))  71 us
    all_gather x1, waiting for transfers between devices, local(): lax.all_gather(delta_curv, 'fsdp', axis=0, tiled=True)  64.4 us
  transfers between devices with their start and end apart: 9, of which 9 were waited for; matrix products, arithmetic and copies ran while one was open for 0% of the time, Pallas kernels for 0%

profile of v1, /device:TPU:14, one launch (start us, length us, event | category | flops | bytes accessed | tf_op | source)
XLA Modules:
  0.0 1273.8 jit_solution(1559684664706206320)
XLA Ops:
  8.0 73.9 %all-gather.8.cloned.1.call-done = bf16[2048,512]{1,0:T(8,128)(2,1)} async-done(((bf16[128,512]{1,0:T(8,128)(2,1)}), bf16[2048,512]{1,0:T(8,128)(2,1)}) %all-gather.8.cloned.1.call-update) | async-done | bytes 2097168 | tf_op jit(solution)/shard_map/all_gather | solution.py:29
  81.8 2.2 fusion.21
  84.1 2.7 convolution_bitcast_fusion
  87.6 108.0 %reduce-scatter.2.cloned.1.call-done = f32[128,512]{0,1:T(8,128)} async-done(((f32[2048,512]{0,1:T(8,128)}), f32[128,512]{0,1:T(8,128)}) %reduce-scatter.2.cloned.1.call-update) | async-done | bytes 262160 | tf_op jit(solution)/shard_map/reduce_scatter | solution.py:38
  195.6 1.1 copy.24
  196.7 0.9 broadcast_multiply_fusion.1
  198.3 298.6 %all-reduce.3.cloned.1.call-done = f32[2,128,512]{2,1,0:T(8,128)} async-done(((f32[2,128,512]{2,1,0:T(8,128)}), f32[2,128,512]{2,1,0:T(8,128)}) %all-reduce.3.cloned.1.call-update) | async-done | bytes 524304 | tf_op jit(solution)/shard_map/psum | solution.py:46
  497.0 1.2 multiply_reduce_fusion.1
  498.2 1.3 subtract_convert_fusion
  499.6 71.0 %all-gather.10.cloned.1.call-done = bf16[2048,512]{1,0:T(8,128)(2,1)} async-done(((bf16[128,512]{1,0:T(8,128)(2,1)}), bf16[2048,512]{1,0:T(8,128)(2,1)}) %all-gather.10.cloned.1.call-update) | async-done | bytes 2097168 | tf_op jit(solution)/shard_map/all_gather | solution.py:49
  570.6 2.8 fusion.10
  573.7 23.3 %all_to_all.19 = bf16[128,16,128]{0,2,1:T(8,128)(2,1)S(1)} all-to-all(bf16[128,16,128]{0,2,1:T(8,128)(2,1)S(1)} %bitcast.45), channel_id=1, replica_groups=mesh['dp'=32,'fsdp'=16] {'fsdp'}, dimensions={1} | all-to-all | bytes 1048576 | tf_op jit(solution)/shard_map/all_to_all | solution.py:30
  597.3 45.4 %all-gather.12.cloned.1.call-done = bf16[2048,512]{1,0:T(8,128)(2,1)} async-done(((bf16[128,512]{1,0:T(8,128)(2,1)}), bf16[2048,512]{1,0:T(8,128)(2,1)}) %all-gather.12.cloned.1.call-update) | async-done | bytes 2097168 | tf_op jit(solution)/shard_map/all_gather | solution.py:53
  642.7 2.3 convolution_bitcast_fusion.3
  645.1 0.9 broadcast_multiply_fusion
  646.1 298.7 %all-reduce.5.cloned.1.call-done = f32[2,128,512]{2,1,0:T(8,128)} async-done(((f32[2,128,512]{2,1,0:T(8,128)}), f32[2,128,512]{2,1,0:T(8,128)}) %all-reduce.5.cloned.1.call-update) | async-done | bytes 524304 | tf_op jit(solution)/shard_map/psum | solution.py:54
  944.8 1.9 multiply_reduce_fusion
  946.7 71.8 %all-gather.14.cloned.1.call-done = bf16[2048,512]{1,0:T(8,128)(2,1)} async-done(((bf16[128,512]{1,0:T(8,128)(2,1)}), bf16[2048,512]{1,0:T(8,128)(2,1)}) %all-gather.14.cloned.1.call-update) | async-done | bytes 2097168 | tf_op jit(solution)/shard_map/all_gather | solution.py:56
  1018.6 2.7 fusion.3
  1021.3 64.4 %all-gather.16.cloned.1.call-done = bf16[2048,512]{1,0:T(8,128)(2,1)} async-done(((bf16[128,512]{1,0:T(8,128)(2,1)}), bf16[2048,512]{1,0:T(8,128)(2,1)}) %all-gather.16.cloned.1.call-update) | async-done | bytes 2097168 | tf_op jit(solution)/shard_map/all_gather | solution.py:60
  1085.7 3.7 fusion.2
  1089.4 170.2 %all-gather.18.cloned.1.call-done = f32[4096,512]{0,1:T(8,128)} async-done(((f32[128,512]{0,1:T(8,128)}), f32[4096,512]{0,1:T(8,128)}) %all-gather.18.cloned.1.call-update) | async-done | bytes 8388624 | tf_op jit(solution)/shard_map/all_gather | solution.py:61
  1259.6 5.2 copy.33
  1264.8 1.6 bitcast_reduce_fusion
  (33 shorter events, 3.4 us)
Async XLA Ops:
  6.5 77.5 %copy-start = (bf16[128,2048]{1,0:T(8,128)(2,1)S(1)}, bf16[128,2048]{1,0:T(8,128)(2,1)}, u32[]{:S(2)}) copy-start(bf16[128,2048]{1,0:T(8,128)(2,1)} %param.6) | copy-start | bytes 1572868
  6.5 77.5 %copy-start.2 = (bf16[128,512]{1,0:T(8,128)(2,1)S(1)}, bf16[128,512]{1,0:T(8,128)(2,1)}, u32[]{:S(2)}) copy-start(bf16[128,512]{1,0:T(8,128)(2,1)} %param.7) | copy-start | bytes 393220
  6.5 75.3 %all-gather.8.cloned.1.call-start = ((), (), s32[]{:S(2)}) async-start(), calls=%async_computation.2 | async-start | bytes 2228224 | tf_op jit(solution)/shard_map/all_gather | solution.py:29
  7.3 188.3 %reduce-scatter.2.cloned.1.call-start = ((), (), s32[]{:S(2)}) async-start(), calls=%async_computation.3 | async-start | bytes 4456448 | tf_op jit(solution)/shard_map/reduce_scatter | solution.py:38
  86.8 110.9 %copy-start.3 = (f32[2]{0:T(128)S(1)}, f32[2]{0:T(128)}, u32[]{:S(2)}) copy-start(f32[2]{0:T(128)} %param.11) | copy-start | bytes 28
  86.8 411.3 %copy-start.1 = (bf16[128,512]{1,0:T(8,128)(2,1)S(1)}, bf16[128,512]{1,0:T(8,128)(2,1)}, u32[]{:S(2)}) copy-start(bf16[128,512]{1,0:T(8,128)(2,1)} %param.8) | copy-start | bytes 393220
  86.8 410.1 %all-reduce.3.cloned.1.call-start = ((), (), s32[]{:S(2)}) async-start(), calls=%async_computation.4 | async-start | bytes 1048576 | tf_op jit(solution)/shard_map/psum | solution.py:46
  197.6 372.9 %all-gather.10.cloned.1.call-start = ((), (), s32[]{:S(2)}) async-start(), calls=%async_computation.5 | async-start | bytes 2228224 | tf_op jit(solution)/shard_map/all_gather | solution.py:49
  499.5 143.2 %all-gather.12.cloned.1.call-start = ((), (), s32[]{:S(2)}) async-start(), calls=%async_computation.6 | async-start | bytes 2228224 | tf_op jit(solution)/shard_map/all_gather | solution.py:53
  573.4 371.5 %all-reduce.5.cloned.1.call-start = ((), (), s32[]{:S(2)}) async-start(), calls=%async_computation.7 | async-start | bytes 1048576 | tf_op jit(solution)/shard_map/psum | solution.py:54
  646.1 372.5 %all-gather.14.cloned.1.call-start = ((), (), s32[]{:S(2)}) async-start(), calls=%async_computation.8 | async-start | bytes 2228224 | tf_op jit(solution)/shard_map/all_gather | solution.py:56
  946.7 139.0 %all-gather.16.cloned.1.call-start = ((), (), s32[]{:S(2)}) async-start(), calls=%async_computation.9 | async-start | bytes 2228224 | tf_op jit(solution)/shard_map/all_gather | solution.py:60
  1021.3 238.3 %all-gather.18.cloned.1.call-start = ((), (), s32[]{:S(2)}) async-start(), calls=%async_computation.10 | async-start | bytes 8650752 | tf_op jit(solution)/shard_map/all_gather | solution.py:61
Sparse Core Ops, SparseCore 0:
  10.6 71.1 all-gather.7
  86.9 108.5 reduce-scatter.1
  198.5 298.4 all-reduce.2
  500.1 70.4 all-gather.9
  573.7 68.9 all-gather.11
  646.2 298.5 all-reduce.4
  948.1 70.4 all-gather.13
  1021.8 63.8 all-gather.15
  1089.5 170.0 all-gather.17
